TPU v7x, 32 devices: a whole 2x2x4 slice. The times are simulated.
32 devices in a mesh: parts: 2 (over y), patch: 4 (over z), sub: 2 (over x), lvl: 2 (over core).
Axes of the slice: x: 2, y: 2, z: 4, core: 2. Of those that a mesh axis runs over, the one named last changes fastest.
Arguments:
- node_states: float32 [8192, 512], P(('parts', 'patch', 'lvl')), parts along dimension 0, may hold values from -6 to 6
- coarse_states: float32 [1024, 512], P(('parts', 'patch', 'lvl')), parts along dimension 0, may hold values from -6 to 6
- children: int32 [512, 7], P(('patch', 'lvl')), may hold values from 0 to 511
- down_sources: int32 [4096, 3], P(('patch', 'lvl')), may hold values from 0 to 63
- bottom_links: int32 [4096, 6], P(('patch', 'lvl')), may hold values from 0 to 767, as said below
- coarse_links: int32 [512, 6], P(('patch', 'lvl')), may hold values from 0 to 511
- upward_sender: float32 [512, 512], P(None, 'sub'), may hold values from -0.25 to 0.25
- upward_receiver: float32 [512, 512], P(None, 'sub'), may hold values from -0.25 to 0.25
- upward_bias: float32 [512], P('sub'), may hold values from -4 to 4
- upward_output: float32 [512, 512], P('sub'), may hold values from -0.25 to 0.25
- upward_gain: float32 [512], replicated, may hold values from 0.1 to 1.9
- coarse_sender: float32 [512, 512], P(None, 'sub'), may hold values from -0.25 to 0.25
- coarse_receiver: float32 [512, 512], P(None, 'sub'), may hold values from -0.25 to 0.25
- coarse_bias: float32 [512], P('sub'), may hold values from -4 to 4
- coarse_output: float32 [512, 512], P('sub'), may hold values from -0.25 to 0.25
- coarse_gain: float32 [512], replicated, may hold values from 0.1 to 1.9
- downward_sender: float32 [512, 512], P(None, 'sub'), may hold values from -0.25 to 0.25
- downward_receiver: float32 [512, 512], P(None, 'sub'), may hold values from -0.25 to 0.25
- downward_bias: float32 [512], P('sub'), may hold values from -4 to 4
- downward_output: float32 [512, 512], P('sub'), may hold values from -0.25 to 0.25
- downward_gain: float32 [512], replicated, may hold values from 0.1 to 1.9
- bottom_sender: float32 [512, 512], P(None, 'sub'), may hold values from -0.25 to 0.25
- bottom_receiver: float32 [512, 512], P(None, 'sub'), may hold values from -0.25 to 0.25
- bottom_bias: float32 [512], P('sub'), may hold values from -4 to 4
- bottom_output: float32 [512, 512], P('sub'), may hold values from -0.25 to 0.25
- bottom_gain: float32 [512], replicated, may hold values from 0.1 to 1.9
Outputs:
- new_nodes: float32 [8192, 512], P(('parts', 'patch', 'lvl')), parts along dimension 0
- new_coarse: float32 [1024, 512], P(('parts', 'patch', 'lvl')), parts along dimension 0
There are 2 independent parts, one for each index of `parts`. A program takes and returns all parts, laid end to end along the dimension named above; an argument that names none is the same for every part. Nothing has to cross between parts.
Inputs may be any that keep to these rules, and one draw needn't show every extreme that they name: bottom_links[n, k] - 128 differs from n's row within its block by at most 128.
All inputs are finite; a program needn't handle non-finite values.
Results may differ from a plain program's by a relative error of at most 0.00011.
Values sent between devices are 32-bit elements; how exact they have to be, the bound alone decides.
A program may use at most 64 MiB of HBM per device.

v0:
```python
import jax
import jax.numpy as jnp
from jax import lax
from jax.sharding import PartitionSpec as P

epsilon = 1e-05
highest = lax.Precision.HIGHEST


def extended(cells, sides, width):
    for axis, dim in sides:
        count = lax.axis_size(axis)
        head = lax.slice_in_dim(cells, 0, width, axis=dim)
        tail = lax.slice_in_dim(cells, cells.shape[dim] - width, cells.shape[dim], axis=dim)
        cells = jnp.concatenate(
            [
                lax.ppermute(tail, axis, [(i, (i + 1) % count) for i in range(count)]),
                cells,
                lax.ppermute(head, axis, [((i + 1) % count, i) for i in range(count)]),
            ],
            axis=dim,
        )
    return cells


def project(states, weights):
    return jnp.dot(states, weights, precision=highest, preferred_element_type=jnp.float32)


def layer_norm(values):
    center = values - jnp.mean(values, axis=-1, keepdims=True)
    spread = jnp.mean(center * center, axis=-1, keepdims=True)
    return center * lax.rsqrt(spread + epsilon)


def hidden_total(picked, receiver_rows):
    return jnp.sum(jax.nn.silu(picked + receiver_rows[:, None, :]), axis=1)


def finish(receivers, hidden, output_weights, gain_vector):
    partial_value = project(hidden, output_weights)
    summed = lax.psum(partial_value, "sub")
    return receivers + gain_vector * layer_norm(summed)


def pick_rows(source_rows, wanted):
    inside = (wanted >= 0) & (wanted < source_rows.shape[0])
    picked = jnp.take(source_rows, jnp.clip(wanted, 0, source_rows.shape[0] - 1), axis=0)
    return jnp.where(inside[:, None], picked, 0.0)


def body(
    node_states,
    coarse_states,
    children,
    down_sources,
    bottom_links,
    coarse_links,
    upward_sender,
    upward_receiver,
    upward_bias,
    upward_output,
    upward_gain,
    coarse_sender,
    coarse_receiver,
    coarse_bias,
    coarse_output,
    coarse_gain,
    downward_sender,
    downward_receiver,
    downward_bias,
    downward_output,
    downward_gain,
    bottom_sender,
    bottom_receiver,
    bottom_bias,
    bottom_output,
    bottom_gain,
):
    sender_rows = project(node_states, upward_sender)
    receiver_rows = project(coarse_states, upward_receiver) + upward_bias
    picked = jnp.take(sender_rows, children, axis=0)
    coarse_up = finish(
        coarse_states, hidden_total(picked, receiver_rows), upward_output, upward_gain
    )
    receiver_rows = project(coarse_up, coarse_receiver) + coarse_bias
    flat_links = coarse_links.reshape(-1)
    own_projection = project(coarse_up, coarse_sender)
    gathered = pick_rows(
        lax.all_gather(own_projection, ("patch", "lvl"), axis=0, tiled=True), flat_links
    )
    picked = gathered.reshape(coarse_links.shape[0], coarse_links.shape[1], receiver_rows.shape[1])
    new_coarse = finish(coarse_up, hidden_total(picked, receiver_rows), coarse_output, coarse_gain)
    sender_rows = project(new_coarse, downward_sender)
    receiver_rows = project(node_states, downward_receiver) + downward_bias
    picked = jnp.take(sender_rows, down_sources, axis=0)
    nodes_down = finish(
        node_states, hidden_total(picked, receiver_rows), downward_output, downward_gain
    )
    rim_rows = node_states.shape[0] // 4
    receiver_rows = project(nodes_down, bottom_receiver) + bottom_bias
    own_projection = project(nodes_down, bottom_sender)
    sender_rows = extended(own_projection, ((("patch", "lvl"), 0),), rim_rows)
    picked = jnp.take(sender_rows, bottom_links, axis=0)
    new_nodes = finish(nodes_down, hidden_total(picked, receiver_rows), bottom_output, bottom_gain)
    return (new_nodes, new_coarse)


def solution(mesh):
    in_specs = (
        P(("parts", "patch", "lvl"), None),
        P(("parts", "patch", "lvl"), None),
        P(("patch", "lvl"), None),
        P(("patch", "lvl"), None),
        P(("patch", "lvl"), None),
        P(("patch", "lvl"), None),
        P(None, "sub"),
        P(None, "sub"),
        P("sub"),
        P("sub", None),
        P(),
        P(None, "sub"),
        P(None, "sub"),
        P("sub"),
        P("sub", None),
        P(),
        P(None, "sub"),
        P(None, "sub"),
        P("sub"),
        P("sub", None),
        P(),
        P(None, "sub"),
        P(None, "sub"),
        P("sub"),
        P("sub", None),
        P(),
    )
    out_specs = (P(("parts", "patch", "lvl"), None), P(("parts", "patch", "lvl"), None))
    return jax.shard_map(body, mesh=mesh, in_specs=in_specs, out_specs=out_specs, check_vma=False)
```

profile of v0, /device:TPU:0, one launch (start us, length us, event | category | flops | bytes accessed | tf_op | source)
XLA Modules:
  0.0 235.3 jit_solution(15321210769861987477)
XLA Ops:
  8.9 2.3 fusion.3
  11.3 1.7 gather_fusion
  14.0 2.1 fusion.4
  16.6 2.0 convolution_add_fusion.1
  18.9 21.8 %all-reduce.5.cloned.1.call-done = f32[64,512]{1,0:T(8,128)} async-done(((f32[64,512]{1,0:T(8,128)}), f32[64,512]{1,0:T(8,128)}) %all-reduce.5.cloned.1.call-update) | async-done | bytes 131088 | tf_op jit(solution)/shard_map/psum | solution.py:42
  40.6 1.0 reduce_sum.109
  41.6 1.1 multiply_reduce_fusion.6
  44.2 14.7 %all_gather.3 = f32[512,256]{1,0:T(8,128)S(1)} all-gather(f32[64,256]{1,0:T(8,128)S(1)} %fusion.5), channel_id=1, replica_groups=mesh['parts'=2,'patch'=4,'sub'=2,'lvl'=2] {'patch','lvl'}, dimensions={0}, use_global_device_ids=true | all-gather | bytes 589824 | tf_op jit(solution)/shard_map/all_gather | solution.py:90
  58.9 1.7 gather_fusion.1
  60.6 1.5 convolution_add_fusion.2
  62.6 2.1 fusion.6
  65.4 21.2 %all-reduce.7.cloned.1.call-done = f32[64,512]{1,0:T(8,128)} async-done(((f32[64,512]{1,0:T(8,128)}), f32[64,512]{1,0:T(8,128)}) %all-reduce.7.cloned.1.call-update) | async-done | bytes 131088 | tf_op jit(solution)/shard_map/psum | solution.py:42
  86.6 1.0 reduce_sum.112
  87.7 1.1 multiply_reduce_fusion.5
  90.2 4.7 %gather_fusion.2 = f32[1536,256]{1,0:T(8,128)} fusion(f32[64,256]{1,0:T(8,128)S(1)} %fusion.7, s32[2048]{0:T(1024)S(1)} %pad_clamp_fusion), kind=kCustom, calls=%fused_computation.2 | custom fusion | bytes 3151872 | tf_op jit(solution)/shard_map/jit(_take)/gather | solution.py:96
  94.9 3.6 %reshape.144 = f32[512,3,256]{2,1,0:T(4,128)} reshape(f32[1536,256]{1,0:T(8,128)} %gather_fusion.2) | data formatting | bytes 3145728 | tf_op jit(solution)/shard_map/jit(_take)/gather | solution.py:96
  98.5 4.4 %fusion = f32[512,256]{1,0:T(8,128)S(1)} fusion(f32[512,3,256]{2,1,0:T(4,128)} %reshape.144, f32[512,256]{1,0:T(8,128)S(1)} %convolution_add_fusion.1, pred[512,3]{1,0:T(8,128)(4,1)S(1)} %copy.33), kind=kLoop, calls=%fused_computation.6 | loop fusion | flops 2621440 | bytes 2622976 | tf_op jit(solution)/shard_map/reduce_sum | solution.py:37
  103.0 2.0 fusion.8
  105.8 39.4 %all-reduce.9.cloned.1.call-done = f32[512,512]{1,0:T(8,128)} async-done(((f32[512,512]{1,0:T(8,128)}), f32[512,512]{1,0:T(8,128)}) %all-reduce.9.cloned.1.call-update) | async-done | bytes 1048592 | tf_op jit(solution)/shard_map/psum | solution.py:42
  145.2 1.4 reduce_sum.115
  146.6 1.5 multiply_reduce_fusion.2
  148.1 1.5 multiply_add_fusion.1
  150.7 3.5 %collective-permute-start.1 = (f32[128,256]{1,0:T(8,128)S(1)}, f32[128,256]{1,0:T(8,128)S(1)}, u32[]{:S(2)}, u32[]{:S(2)}) collective-permute-start(f32[128,256]{1,0:T(8,128)S(1)} %get-tuple-element.3), channel_id=1, source_target_pairs={{1,0},{4,1},{5,4},{8,5},{9,8},{12,9},{13,12},{0,13},{3,2},{6,3},{7... | collective-permute-start | bytes 393224 | tf_op jit(solution)/shard_map/ppermute | solution.py:19
  155.3 1.7 collective-permute-done
  157.1 12.3 %gather_fusion.3 = f32[3072,256]{1,0:T(8,128)} fusion(f32[768,256]{1,0:T(8,128)S(1)} %pad_maximum_fusion, s32[3072]{0:T(1024)S(1)} %broadcast_clamp_fusion), kind=kCustom, calls=%fused_computation.3 | custom fusion | bytes 6303744 | tf_op jit(solution)/shard_map/jit(_take)/gather | solution.py:104
  169.4 4.5 %reshape.152 = f32[512,6,256]{2,1,0:T(8,128)} reshape(f32[3072,256]{1,0:T(8,128)} %gather_fusion.3) | data formatting | bytes 6291456 | tf_op jit(solution)/shard_map/jit(_take)/gather | solution.py:104
  173.9 7.1 %multiply_reduce_fusion = f32[512,256]{1,0:T(8,128)S(1)} fusion(f32[512,6,256]{2,1,0:T(8,128)} %reshape.152, f32[512,256]{1,0:T(8,128)S(1)} %convolution_add_fusion, pred[512,6]{1,0:T(8,128)(4,1)S(1)} %copy.40), kind=kLoop, calls=%fused_computation.4 | loop fusion | flops 5373952 | bytes 4197376 | tf_op jit(solution)/shard_map/reduce_sum | solution.py:37
  181.1 2.0 fusion.10
  183.1 40.4 %all-reduce.11.cloned.1.call-done = f32[512,512]{1,0:T(8,128)} async-done(((f32[512,512]{1,0:T(8,128)}), f32[512,512]{1,0:T(8,128)}) %all-reduce.11.cloned.1.call-update) | async-done | bytes 1048592 | tf_op jit(solution)/shard_map/psum | solution.py:42
  223.5 1.4 reduce_sum.118
  224.9 1.5 multiply_reduce_fusion.1
  226.4 2.4 %multiply_add_fusion = f32[512,512]{1,0:T(8,128)} fusion(f32[512,512]{1,0:T(8,128)S(1)} %multiply_add_fusion.1, f32[512,512]{1,0:T(8,128)} %all-reduce.11.cloned.1.call-done, f32[512]{0:T(512)S(1)} %add_rsqrt_fusion, f32[512]{0:T(512)S(1)} %broadcast_multiply_fusion, f32[512]{0:T(512)S(1)} %copy-done.16), kind=kLoop, calls=%fused_computation.11 | loop fusion | flops 1048576 | bytes 3151872 | tf_op jit(solution)/shard_map/add | solution.py:43
  (99 shorter events, 10.1 us)
Async XLA Ops:
  7.2 95.8 %copy-start = (f32[256,512]{1,0:T(8,128)S(1)}, f32[256,512]{1,0:T(8,128)}, u32[]{:S(2)}) copy-start(f32[256,512]{1,0:T(8,128)} %param.45) | copy-start | bytes 1572868
  7.2 33.4 %all-reduce.5.cloned.1.call-start = ((), (), s32[]{:S(2)}) async-start(), calls=%async_computation | async-start | bytes 262144 | tf_op jit(solution)/shard_map/psum | solution.py:42
  11.3 2.0 copy-start.2
  11.3 2.0 copy-start.5
  11.3 2.0 copy-start.17
  11.3 4.9 %copy-start.12 = (s32[64,6]{0,1:T(8,128)S(1)}, s32[64,6]{0,1:T(8,128)}, u32[]{:S(2)}) copy-start(s32[64,6]{0,1:T(8,128)} %param.31) | copy-start | bytes 4612
  11.3 5.2 %copy-start.11 = (s32[512,3]{0,1:T(4,128)S(1)}, s32[512,3]{0,1:T(4,128)}, u32[]{:S(2)}) copy-start(s32[512,3]{0,1:T(4,128)} %param.29) | copy-start | bytes 18436
  11.3 5.2 %copy-start.1 = (f32[512,512]{1,0:T(8,128)S(1)}, f32[512,512]{1,0:T(8,128)}, u32[]{:S(2)}) copy-start(f32[512,512]{1,0:T(8,128)} %param.26) | copy-start | bytes 3145732
  11.3 5.2 %copy-start.18 = (f32[256]{0:T(256)S(1)}, f32[256]{0:T(256)}, u32[]{:S(2)}) copy-start(f32[256]{0:T(256)} %param.44) | copy-start | bytes 3076
  13.1 29.7 %copy-start.13 = (f32[512]{0:T(512)S(1)}, f32[512]{0:T(512)}, u32[]{:S(2)}) copy-start(f32[512]{0:T(512)} %param.36) | copy-start | bytes 6148
  13.7 30.1 %copy-start.3 = (f32[512,256]{1,0:T(8,128)S(1)}, f32[512,256]{1,0:T(8,128)}, u32[]{:S(2)}) copy-start(f32[512,256]{1,0:T(8,128)} %param.37) | copy-start | bytes 1572868
  16.2 70.4 %all-reduce.7.cloned.1.call-start = ((), (), s32[]{:S(2)}) async-start(), calls=%async_computation.1 | async-start | bytes 262144 | tf_op jit(solution)/shard_map/psum | solution.py:42
  41.6 19.0 %copy-start.19 = (f32[256]{0:T(256)S(1)}, f32[256]{0:T(256)}, u32[]{:S(2)}) copy-start(f32[256]{0:T(256)} %param.39) | copy-start | bytes 3076
  58.9 29.9 %copy-start.14 = (f32[512]{0:T(512)S(1)}, f32[512]{0:T(512)}, u32[]{:S(2)}) copy-start(f32[512]{0:T(512)} %param.41) | copy-start | bytes 6148
  60.6 29.2 %copy-start.4 = (f32[512,256]{1,0:T(8,128)S(1)}, f32[512,256]{1,0:T(8,128)}, u32[]{:S(2)}) copy-start(f32[512,256]{1,0:T(8,128)} %param.42) | copy-start | bytes 1572868
  64.8 80.5 %all-reduce.9.cloned.1.call-start = ((), (), s32[]{:S(2)}) async-start(), calls=%async_computation.2 | async-start | bytes 2097152 | tf_op jit(solution)/shard_map/psum | solution.py:42
  89.8 5.1 %copy-start.6 = (f32[64,512]{1,0:T(8,128)}, f32[64,512]{1,0:T(8,128)S(1)}, u32[]{:S(2)}) copy-start(f32[64,512]{1,0:T(8,128)S(1)} %multiply_add_fusion.2) | copy-start | bytes 393220
  98.5 6.7 %copy-start.10 = (s32[512,6]{0,1:T(8,128)S(1)}, s32[512,6]{0,1:T(8,128)}, u32[]{:S(2)}) copy-start(s32[512,6]{0,1:T(8,128)} %param.30) | copy-start | bytes 36868
  102.9 45.2 %copy-start.15 = (f32[512]{0:T(512)S(1)}, f32[512]{0:T(512)}, u32[]{:S(2)}) copy-start(f32[512]{0:T(512)} %param.46) | copy-start | bytes 6148
  105.0 44.7 %copy-start.7 = (f32[512,256]{1,0:T(8,128)S(1)}, f32[512,256]{1,0:T(8,128)}, u32[]{:S(2)}) copy-start(f32[512,256]{1,0:T(8,128)} %param.47) | copy-start | bytes 1572868
  105.0 118.5 %all-reduce.11.cloned.1.call-start = ((), (), s32[]{:S(2)}) async-start(), calls=%async_computation.3 | async-start | bytes 2097152 | tf_op jit(solution)/shard_map/psum | solution.py:42
  148.1 6.2 %copy-start.8 = (f32[512,256]{1,0:T(8,128)S(1)}, f32[512,256]{1,0:T(8,128)}, u32[]{:S(2)}) copy-start(f32[512,256]{1,0:T(8,128)} %param.48) | copy-start | bytes 1572868
  148.1 6.2 %copy-start.20 = (f32[256]{0:T(256)S(1)}, f32[256]{0:T(256)}, u32[]{:S(2)}) copy-start(f32[256]{0:T(256)} %param.49) | copy-start | bytes 3076
  150.7 6.3 %collective-permute-start = (f32[128,256]{1,0:T(8,128)S(1)}, f32[128,256]{1,0:T(8,128)S(1)}, u32[]{:S(2)}, u32[]{:S(2)}) collective-permute-start(f32[128,256]{1,0:T(8,128)S(1)} %get-tuple-element.2), channel_id=1, source_target_pairs={{0,1},{1,4},{4,5},{5,8},{8,9},{9,12},{12,13},{13,0},{2,3},{3,6},{6... | collective-permute-start | bytes 393224 | tf_op jit(solution)/shard_map/ppermute | solution.py:17
  150.7 6.3 %collective-permute-start.1 = (f32[128,256]{1,0:T(8,128)S(1)}, f32[128,256]{1,0:T(8,128)S(1)}, u32[]{:S(2)}, u32[]{:S(2)}) collective-permute-start(f32[128,256]{1,0:T(8,128)S(1)} %get-tuple-element.3), channel_id=1, source_target_pairs={{1,0},{4,1},{5,4},{8,5},{9,8},{12,9},{13,12},{0,13},{3,2},{6,3},{7... | collective-permute-start | bytes 393224 | tf_op jit(solution)/shard_map/ppermute | solution.py:19
  173.9 7.1 %copy-start.9 = (f32[256,512]{1,0:T(8,128)S(1)}, f32[256,512]{1,0:T(8,128)}, u32[]{:S(2)}) copy-start(f32[256,512]{1,0:T(8,128)} %param.50) | copy-start | bytes 1572868
  181.1 45.3 %copy-start.16 = (f32[512]{0:T(512)S(1)}, f32[512]{0:T(512)}, u32[]{:S(2)}) copy-start(f32[512]{0:T(512)} %param.51) | copy-start | bytes 6148
Sparse Core Ops, SparseCore 0:
  16.3 24.2 all-reduce.4
  64.9 21.6 all-reduce.6
  105.1 40.0 all-reduce.8
  183.2 40.2 all-reduce.10
where the time goes:
time: 236 us; the launch traced here: 235 us
  waiting for transfers between devices  125 us (53%)
  local copies, waits for them, and re-layouts  30.7 us (13%)
  other arithmetic  29.8 us (13%)
  matrix products  17.2 us (7%)
  blocking collectives  14.7 us (6%)
  between operations  14.4 us (6%)
  starting transfers between devices  3.93 us (2%)
    psum x4, waiting for transfers between devices, finish(): summed = lax.psum(partial_value, 'sub')  123 us
    dot_general x12, matrix products, project(): jnp.dot(states, weights, precision=highest, preferred_element_type=jnp.fl...  17.2 us
    gather x2, local copies, waits for them, and re-layouts, body(): picked = jnp.take(sender_rows, bottom_links, axis=0)  16.9 us
    all_gather x1, blocking collectives, body(): lax.all_gather(own_projection, ('patch', 'lvl'), axis=0, tiled=True)  14.7 us
    reduce_sum x4, other arithmetic, hidden_total(): return jnp.sum(jax.nn.silu(picked + receiver_rows[:, None, :]), axis=1)  12.4 us
    gather x2, local copies, waits for them, and re-layouts, body(): picked = jnp.take(sender_rows, down_sources, axis=0)  8.31 us
    add x4, other arithmetic, finish(): return receivers + gain_vector * layer_norm(summed)  5.93 us
    reduce_sum x4, other arithmetic, layer_norm(): spread = jnp.mean(center * center, axis=-1, keepdims=True)  5.13 us
  transfers between devices with their start and end apart: 6, of which 5 were waited for; matrix products, arithmetic and copies ran while one was open for 2% of the time, Pallas kernels for 0%

commit v1 on v0

--- a/solution.py
+++ b/solution.py
@@ -39,7 +39,7 @@
 
 def finish(receivers, hidden, output_weights, gain_vector):
     partial_value = project(hidden, output_weights)
-    summed = lax.psum(partial_value, "sub")
+    summed = jnp.sum(lax.all_gather(partial_value, "sub"), axis=0)
     return receivers + gain_vector * layer_norm(summed)
 
 

time: 236 us -> 184 us (0.78)
  waiting for transfers between devices: 125 us -> 68.7 us
  blocking collectives: 14.7 us -> 28.8 us
  matrix products: 17.2 us -> 12.9 us
  other arithmetic: 29.8 us -> 26.8 us
  local copies, waits for them, and re-layouts: 30.7 us -> 28 us
    psum x4 -> x0, waiting for transfers between devices: 123 us -> none  [finish(): summed = lax.psum(partial_value, 'sub')]
    all_gather x0 -> x2, waiting for transfers between devices: none -> 66.9 us  [finish(): summed = jnp.sum(lax.all_gather(partial_value, 'sub'), axis=0)]
    all_gather x0 -> x2, blocking collectives: none -> 13.5 us  [finish(): summed = jnp.sum(lax.all_gather(partial_value, 'sub'), axis=0)]
    dot_general x12, matrix products: 17.2 us -> 12.9 us  [project(): jnp.dot(states, weights, precision=highest, preferred_element_type=jnp.fl...]
    reduce_sum x4, other arithmetic: 5.13 us -> 0.87 us  [layer_norm(): spread = jnp.mean(center * center, axis=-1, keepdims=True)]
    reduce_sum x0 -> x4, other arithmetic: none -> 3.83 us  [finish(): summed = jnp.sum(lax.all_gather(partial_value, 'sub'), axis=0)]
    add x4, other arithmetic: 5.93 us -> 2.85 us  [finish(): return receivers + gain_vector * layer_norm(summed)]
    gather x2, local copies, waits for them, and re-layouts: 8.31 us -> 5.41 us  [body(): picked = jnp.take(sender_rows, down_sources, axis=0)]
  transfers between devices with their start and end apart: 6 -> 4, of which waited for: 5 -> 3; matrix products, arithmetic and copies ran while one was open for 2% -> 1% of each run, Pallas kernels for 0% -> 0%
where the time goes in v1:
time: 184 us
  waiting for transfers between devices  68.7 us (37%)
  blocking collectives  28.8 us (16%)
  local copies, waits for them, and re-layouts  28 us (15%)
  other arithmetic  26.8 us (15%)
  between operations  14.7 us (8%)
  matrix products  12.9 us (7%)
  starting transfers between devices  3.85 us (2%)
    all_gather x2, waiting for transfers between devices, finish(): summed = jnp.sum(lax.all_gather(partial_value, 'sub'), axis=0)  66.9 us
    gather x2, local copies, waits for them, and re-layouts, body(): picked = jnp.take(sender_rows, bottom_links, axis=0)  16.9 us
    all_gather x1, blocking collectives, body(): lax.all_gather(own_projection, ('patch', 'lvl'), axis=0, tiled=True)  15.3 us
    all_gather x2, blocking collectives, finish(): summed = jnp.sum(lax.all_gather(partial_value, 'sub'), axis=0)  13.5 us
    dot_general x12, matrix products, project(): jnp.dot(states, weights, precision=highest, preferred_element_type=jnp.fl...  12.9 us
    reduce_sum x4, other arithmetic, hidden_total(): return jnp.sum(jax.nn.silu(picked + receiver_rows[:, None, :]), axis=1)  11 us
    gather x2, local copies, waits for them, and re-layouts, body(): picked = jnp.take(sender_rows, down_sources, axis=0)  5.41 us
    reduce_sum x8, other arithmetic, layer_norm(): center = values - jnp.mean(values, axis=-1, keepdims=True)  3.91 us
  transfers between devices with their start and end apart: 4, of which 3 were waited for; matrix products, arithmetic and copies ran while one was open for 1% of the time, Pallas kernels for 0%

profile of v1, /device:TPU:0, one launch (start us, length us, event | category | flops | bytes accessed | tf_op | source)
XLA Modules:
  0.0 183.8 jit_solution(10161168155501723928)
XLA Ops:
  7.2 0.7 compare_select_fusion.3
  8.0 0.7 compare_and_fusion.4
  9.3 0.7 compare_and_fusion.3
  10.0 0.7 compare_select_fusion.1
  10.7 0.7 compare_and_fusion.1
  11.7 2.3 %fusion.3 = f32[512,256]{1,0:T(8,128)S(1)} fusion(f32[512,512]{1,0:T(8,128)} %param.26, f32[512,256]{1,0:T(8,128)} %param.32), kind=kOutput, calls=%fused_computation.47 | convolution fusion | flops 805306368 | bytes 2097152 | tf_op jit(solution)/shard_map/dot_general | solution.py:27
  14.1 1.7 gather_fusion
  17.3 7.1 %all-gather = f32[128,512]{1,0:T(8,128)S(1)} all-gather(f32[64,512]{1,0:T(8,128)S(1)} %fusion.4), channel_id=2, replica_groups=mesh['parts'=2,'patch'=4,'sub'=2,'lvl'=2] {'sub'}, dimensions={0}, use_global_device_ids=true | all-gather | bytes 393216 | tf_op jit(solution)/shard_map/all_gather | solution.py:42
  25.4 15.3 %all_gather.29 = f32[512,256]{1,0:T(8,128)S(1)} all-gather(f32[64,256]{1,0:T(8,128)S(1)} %fusion.5), channel_id=1, replica_groups=mesh['parts'=2,'patch'=4,'sub'=2,'lvl'=2] {'patch','lvl'}, dimensions={0}, use_global_device_ids=true | all-gather | bytes 589824 | tf_op jit(solution)/shard_map/all_gather | solution.py:90
  41.0 1.7 gather_fusion.1
  44.3 6.4 %all-gather.1 = f32[128,512]{1,0:T(8,128)S(1)} all-gather(f32[64,512]{1,0:T(8,128)S(1)} %fusion.6), channel_id=3, replica_groups=mesh['parts'=2,'patch'=4,'sub'=2,'lvl'=2] {'sub'}, dimensions={0}, use_global_device_ids=true | all-gather | bytes 393216 | tf_op jit(solution)/shard_map/all_gather | solution.py:42
  52.1 3.7 %gather_fusion.2 = f32[1536,256]{1,0:T(8,128)S(1)} fusion(f32[64,256]{1,0:T(8,128)S(1)} %fusion.7, s32[2048]{0:T(1024)S(1)} %pad_clamp_fusion), kind=kCustom, calls=%fused_computation.2 | custom fusion | bytes 3151872 | tf_op jit(solution)/shard_map/jit(_take)/gather | solution.py:96
  55.8 1.7 reshape.144
  57.7 2.2 %convolution_add_fusion.1 = f32[512,256]{1,0:T(8,128)S(1)} fusion(f32[512,512]{1,0:T(8,128)S(1)} %copy-done.1, f32[512,256]{1,0:T(8,128)} %param.43, f32[256]{0:T(256)S(1)} %copy-done.21), kind=kOutput, calls=%fused_computation.8 | convolution fusion | flops 805437440 | bytes 2098176 | tf_op jit(solution)/shard_map/dot_general | solution.py:27
  59.9 3.1 %fusion = f32[512,256]{1,0:T(8,128)S(1)} fusion(f32[512,3,256]{2,1,0:T(4,128)S(1)} %copy-done.2, f32[512,256]{1,0:T(8,128)S(1)} %convolution_add_fusion.1, pred[512,3]{1,0:T(8,128)(4,1)S(1)} %copy.42), kind=kLoop, calls=%fused_computation.6 | loop fusion | flops 2621440 | bytes 2622976 | tf_op jit(solution)/shard_map/reduce_sum | solution.py:37
  63.0 2.0 %fusion.8 = f32[512,512]{1,0:T(8,128)} fusion(f32[512,256]{1,0:T(8,128)S(1)} %fusion, f32[256,512]{1,0:T(8,128)S(1)} %copy-done), kind=kOutput, calls=%fused_computation.52 | convolution fusion | flops 805306368 | bytes 2097152 | tf_op jit(solution)/shard_map/dot_general | solution.py:27
  65.8 33.5 %all-gather.7.cloned.1.call-done = f32[1024,512]{1,0:T(8,128)} async-done(((f32[512,512]{1,0:T(8,128)}), f32[1024,512]{1,0:T(8,128)}) %all-gather.7.cloned.1.call-update) | async-done | bytes 2097168 | tf_op jit(solution)/shard_map/all_gather | solution.py:42
  99.3 1.9 %reduce_sum.153 = f32[512,512]{1,0:T(8,128)S(1)} reduce(f32[2,512,512]{2,1,0:T(8,128)} %bitcast.28, f32[]{:T(128)} %constant.80.clone.1), dimensions={0}, to_apply=%region_9.10 | reduce | flops 262144 | bytes 3145732 | tf_op jit(solution)/shard_map/reduce_sum | solution.py:42
  101.2 1.8 reduce.8
  103.4 1.5 multiply_add_fusion.1
  104.9 1.0 fusion.9
  106.0 3.5 %collective-permute-start.1 = (f32[128,256]{1,0:T(8,128)S(1)}, f32[128,256]{1,0:T(8,128)S(1)}, u32[]{:S(2)}, u32[]{:S(2)}) collective-permute-start(f32[128,256]{1,0:T(8,128)S(1)} %get-tuple-element.3), channel_id=1, source_target_pairs={{1,0},{4,1},{5,4},{8,5},{9,8},{12,9},{13,12},{0,13},{3,2},{6,3},{7... | collective-permute-start | bytes 393224 | tf_op jit(solution)/shard_map/ppermute | solution.py:19
  109.5 1.0 convolution_add_fusion
  110.5 1.7 collective-permute-done
  112.3 12.3 %gather_fusion.3 = f32[3072,256]{1,0:T(8,128)} fusion(f32[768,256]{1,0:T(8,128)S(1)} %pad_maximum_fusion, s32[3072]{0:T(1024)S(1)} %broadcast_clamp_fusion), kind=kCustom, calls=%fused_computation.3 | custom fusion | bytes 6303744 | tf_op jit(solution)/shard_map/jit(_take)/gather | solution.py:104
  124.6 4.5 %reshape.152 = f32[512,6,256]{2,1,0:T(8,128)} reshape(f32[3072,256]{1,0:T(8,128)} %gather_fusion.3) | data formatting | bytes 6291456 | tf_op jit(solution)/shard_map/jit(_take)/gather | solution.py:104
  129.2 7.1 %multiply_reduce_fusion = f32[512,256]{1,0:T(8,128)S(1)} fusion(f32[512,6,256]{2,1,0:T(8,128)} %reshape.152, f32[512,256]{1,0:T(8,128)S(1)} %convolution_add_fusion, pred[512,6]{1,0:T(8,128)(4,1)S(1)} %copy.49), kind=kLoop, calls=%fused_computation.4 | loop fusion | flops 5373952 | bytes 4197376 | tf_op jit(solution)/shard_map/reduce_sum | solution.py:37
  136.3 2.0 %fusion.10 = f32[512,512]{1,0:T(8,128)} fusion(f32[512,256]{1,0:T(8,128)S(1)} %multiply_reduce_fusion, f32[256,512]{1,0:T(8,128)S(1)} %copy-done.13), kind=kOutput, calls=%fused_computation.54 | convolution fusion | flops 805306368 | bytes 2097152 | tf_op jit(solution)/shard_map/dot_general | solution.py:27
  138.3 33.4 %all-gather.9.cloned.1.call-done = f32[1024,512]{1,0:T(8,128)} async-done(((f32[512,512]{1,0:T(8,128)}), f32[1024,512]{1,0:T(8,128)}) %all-gather.9.cloned.1.call-update) | async-done | bytes 2097168 | tf_op jit(solution)/shard_map/all_gather | solution.py:42
  171.7 1.9 %reduce_sum.157 = f32[512,512]{1,0:T(8,128)S(1)} reduce(f32[2,512,512]{2,1,0:T(8,128)} %bitcast.29, f32[]{:T(128)} %constant.80.clone.1), dimensions={0}, to_apply=%region_13.14 | reduce | flops 262144 | bytes 3145732 | tf_op jit(solution)/shard_map/reduce_sum | solution.py:42
  173.6 1.8 reduce.10
  175.7 1.2 multiply_add_fusion
  (111 shorter events, 8.2 us)
Async XLA Ops:
  7.2 55.8 %copy-start = (f32[256,512]{1,0:T(8,128)S(1)}, f32[256,512]{1,0:T(8,128)}, u32[]{:S(2)}) copy-start(f32[256,512]{1,0:T(8,128)} %param.45) | copy-start | bytes 1572868
  7.2 92.2 %all-gather.7.cloned.1.call-start = ((), (), s32[]{:S(2)}) async-start(), calls=%async_computation | async-start | bytes 3145728 | tf_op jit(solution)/shard_map/all_gather | solution.py:42
  14.0 2.0 %copy-start.3 = (f32[512,256]{1,0:T(8,128)S(1)}, f32[512,256]{1,0:T(8,128)}, u32[]{:S(2)}) copy-start(f32[512,256]{1,0:T(8,128)} %param.33) | copy-start | bytes 1572868
  14.1 2.0 %copy-start.9 = (f32[64,512]{1,0:T(8,128)S(1)}, f32[64,512]{1,0:T(8,128)}, u32[]{:S(2)}) copy-start(f32[64,512]{1,0:T(8,128)} %param.27) | copy-start | bytes 393220
  14.1 2.0 %copy-start.19 = (f32[256]{0:T(256)S(1)}, f32[256]{0:T(256)}, u32[]{:S(2)}) copy-start(f32[256]{0:T(256)} %param.34) | copy-start | bytes 3076
  15.8 1.0 copy-start.4
  15.8 9.0 %copy-start.15 = (f32[512]{0:T(512)S(1)}, f32[512]{0:T(512)}, u32[]{:S(2)}) copy-start(f32[512]{0:T(512)} %param.36) | copy-start | bytes 6148
  15.9 9.1 %copy-start.5 = (f32[512,256]{1,0:T(8,128)S(1)}, f32[512,256]{1,0:T(8,128)}, u32[]{:S(2)}) copy-start(f32[512,256]{1,0:T(8,128)} %param.37) | copy-start | bytes 1572868
  40.9 2.0 %copy-start.6 = (f32[512,256]{1,0:T(8,128)S(1)}, f32[512,256]{1,0:T(8,128)}, u32[]{:S(2)}) copy-start(f32[512,256]{1,0:T(8,128)} %param.38) | copy-start | bytes 1572868
  40.9 2.0 %copy-start.20 = (f32[256]{0:T(256)S(1)}, f32[256]{0:T(256)}, u32[]{:S(2)}) copy-start(f32[256]{0:T(256)} %param.39) | copy-start | bytes 3076
  41.0 2.9 %copy-start.7 = (f32[256,512]{1,0:T(8,128)S(1)}, f32[256,512]{1,0:T(8,128)}, u32[]{:S(2)}) copy-start(f32[256,512]{1,0:T(8,128)} %param.40) | copy-start | bytes 1572868
  42.7 8.8 %copy-start.16 = (f32[512]{0:T(512)S(1)}, f32[512]{0:T(512)}, u32[]{:S(2)}) copy-start(f32[512]{0:T(512)} %param.41) | copy-start | bytes 6148
  43.0 8.7 %copy-start.8 = (f32[512,256]{1,0:T(8,128)S(1)}, f32[512,256]{1,0:T(8,128)}, u32[]{:S(2)}) copy-start(f32[512,256]{1,0:T(8,128)} %param.42) | copy-start | bytes 1572868
  51.7 4.1 %copy-start.10 = (f32[64,512]{1,0:T(8,128)}, f32[64,512]{1,0:T(8,128)S(1)}, u32[]{:S(2)}) copy-start(f32[64,512]{1,0:T(8,128)S(1)} %multiply_add_fusion.2) | copy-start | bytes 393220
  55.8 2.0 %copy-start.1 = (f32[512,512]{1,0:T(8,128)S(1)}, f32[512,512]{1,0:T(8,128)}, u32[]{:S(2)}) copy-start(f32[512,512]{1,0:T(8,128)} %param.26) | copy-start | bytes 3145732
  55.8 2.0 %copy-start.21 = (f32[256]{0:T(256)S(1)}, f32[256]{0:T(256)}, u32[]{:S(2)}) copy-start(f32[256]{0:T(256)} %param.44) | copy-start | bytes 3076
  57.7 2.2 %copy-start.2 = (f32[512,3,256]{2,1,0:T(4,128)S(1)}, f32[512,3,256]{2,1,0:T(4,128)}, u32[]{:S(2)}) copy-start(f32[512,3,256]{2,1,0:T(4,128)} %reshape.144) | copy-start | bytes 4718596
  63.0 2.3 %copy-start.14 = (s32[512,6]{0,1:T(8,128)S(1)}, s32[512,6]{0,1:T(8,128)}, u32[]{:S(2)}) copy-start(s32[512,6]{0,1:T(8,128)} %param.30) | copy-start | bytes 36868
  65.0 106.7 %all-gather.9.cloned.1.call-start = ((), (), s32[]{:S(2)}) async-start(), calls=%async_computation.1 | async-start | bytes 3145728 | tf_op jit(solution)/shard_map/all_gather | solution.py:42
  101.2 2.1 %copy-start.17 = (f32[512]{0:T(512)S(1)}, f32[512]{0:T(512)}, u32[]{:S(2)}) copy-start(f32[512]{0:T(512)} %param.46) | copy-start | bytes 6148
  103.1 1.8 copy-start.11
  104.9 4.6 %copy-start.12 = (f32[512,256]{1,0:T(8,128)S(1)}, f32[512,256]{1,0:T(8,128)}, u32[]{:S(2)}) copy-start(f32[512,256]{1,0:T(8,128)} %param.48) | copy-start | bytes 1572868
  104.9 4.6 %copy-start.22 = (f32[256]{0:T(256)S(1)}, f32[256]{0:T(256)}, u32[]{:S(2)}) copy-start(f32[256]{0:T(256)} %param.49) | copy-start | bytes 3076
  105.9 6.3 %collective-permute-start = (f32[128,256]{1,0:T(8,128)S(1)}, f32[128,256]{1,0:T(8,128)S(1)}, u32[]{:S(2)}, u32[]{:S(2)}) collective-permute-start(f32[128,256]{1,0:T(8,128)S(1)} %get-tuple-element.2), channel_id=1, source_target_pairs={{0,1},{1,4},{4,5},{5,8},{8,9},{9,12},{12,13},{13,0},{2,3},{3,6},{6... | collective-permute-start | bytes 393224 | tf_op jit(solution)/shard_map/ppermute | solution.py:17
  106.0 6.3 %collective-permute-start.1 = (f32[128,256]{1,0:T(8,128)S(1)}, f32[128,256]{1,0:T(8,128)S(1)}, u32[]{:S(2)}, u32[]{:S(2)}) collective-permute-start(f32[128,256]{1,0:T(8,128)S(1)} %get-tuple-element.3), channel_id=1, source_target_pairs={{1,0},{4,1},{5,4},{8,5},{9,8},{12,9},{13,12},{0,13},{3,2},{6,3},{7... | collective-permute-start | bytes 393224 | tf_op jit(solution)/shard_map/ppermute | solution.py:19
  129.2 7.1 %copy-start.13 = (f32[256,512]{1,0:T(8,128)S(1)}, f32[256,512]{1,0:T(8,128)}, u32[]{:S(2)}) copy-start(f32[256,512]{1,0:T(8,128)} %param.50) | copy-start | bytes 1572868
  173.6 2.1 %copy-start.18 = (f32[512]{0:T(512)S(1)}, f32[512]{0:T(512)}, u32[]{:S(2)}) copy-start(f32[512]{0:T(512)} %param.51) | copy-start | bytes 6148
Sparse Core Ops, SparseCore 0:
  65.2 34.1 all-gather.6
  138.4 33.2 all-gather.8
